TPU v7x, 32 devices: a whole 2x2x4 slice. The times are simulated.
32 devices in a mesh: ctx: 8 (over y, x, core), fsdp: 4 (over z).
Axes of the slice: x: 2, y: 2, z: 4, core: 2. Of those that a mesh axis runs over, the one named last changes fastest.
Arguments:
- inner: bfloat16 [16384, 8192], P('ctx', 'fsdp'), may hold values from -6 to 6
- proj_weight: bfloat16 [32, 8192], P(None, 'fsdp'), may hold values from -0.0625 to 0.0625
- rates: float32 [8192], P('fsdp'), may hold values from 3.0517578e-06 to 0.0333333333
- keep: float32 [16384], P('ctx'), may hold values from 0.216 to 1, as said below
- skip: float32 [8192], P('fsdp'), may hold values from 0.5 to 1.5
- upstream: bfloat16 [16384, 8192], P('ctx', 'fsdp'), may hold values from -6 to 6
Outputs:
- input_grad: bfloat16 [16384, 8192], P('ctx', 'fsdp')
- proj_grad: float32 [32, 8192], P(None, 'fsdp')
Inputs may be any that keep to these rules, and one draw needn't show every extreme that they name: `keep`: factors on the tokens' decays.
All inputs are finite; a program needn't handle non-finite values.
Results may differ from a plain program's by a relative error of at most 0.0058.
Values sent between devices are 32-bit elements; how exact they have to be, the bound alone decides.
A program may use at most 128 MiB of HBM per device.

v0:
```python
import jax
import jax.numpy as jnp
from jax import lax
from jax.sharding import PartitionSpec as P

BLK = 256


def carried_in(shard, axis, combine, identity, reverse):
    length, place = (lax.axis_size(axis), lax.axis_index(axis))
    everything = jax.tree.map(lambda part: lax.all_gather(part, axis), shard)
    start = jax.tree.map(
        lambda part, zero: jnp.broadcast_to(jnp.asarray(zero, part.dtype), part.shape),
        shard,
        identity,
    )

    def step(k, before):
        at = length - 1 - k if reverse else k
        reached = at > place if reverse else at < place
        new = combine(before, jax.tree.map(lambda part: part[at], everything))
        return jax.tree.map(lambda a, b: jnp.where(reached, a, b), new, before)

    return lax.fori_loop(0, length, step, start)


def batched(form, left, right):
    return jnp.einsum(form, left, right, preferred_element_type=jnp.float32)


def precise(form, left, right):
    return jnp.einsum(
        form, left, right, precision=lax.Precision.HIGHEST, preferred_element_type=jnp.float32
    )


def combine(earlier, later):
    return (earlier[0] * later[0], later[1] + later[0][None, :] * earlier[1])


def local(inner, proj_weight, rates, keep, skip, upstream):
    length = inner.shape[0]
    channels = inner.shape[1]
    nstate = proj_weight.shape[0] // 2
    nblocks = length // BLK
    partial_coef = lax.dot_general(
        inner, proj_weight, (((1,), (1,)), ((), ())), preferred_element_type=jnp.float32
    )
    coeffs = lax.psum(partial_coef, "fsdp")
    coef_wide = coeffs.reshape(nblocks, BLK, 2 * nstate)
    write_wide = coef_wide[:, :, :nstate]
    read_wide = coef_wide[:, :, nstate:]
    coef_blocks = coeffs.astype(jnp.bfloat16).reshape(nblocks, BLK, 2 * nstate)
    write_coef = coef_blocks[:, :, :nstate]
    read_coef = coef_blocks[:, :, nstate:]
    factor = 1.0 / jnp.sqrt(jnp.float32(nstate))
    input_scale = jnp.sqrt(-jnp.expm1(-2.0 * rates))
    offsets = jnp.arange(1, BLK + 1).astype(jnp.float32)
    within_base = jnp.exp(-offsets[:, None] * rates[None, :])
    within = within_base[None] * jnp.cumprod(keep.reshape(nblocks, BLK), axis=1)[:, :, None]
    upstream_f = upstream.astype(jnp.float32).reshape(nblocks, BLK, channels)
    scaled = (
        input_scale[None, None, :]
        * inner.astype(jnp.float32).reshape(nblocks, BLK, channels)
        / within
    ).astype(jnp.bfloat16)
    weighted = (within * upstream_f).astype(jnp.bfloat16)
    decays = within[:, -1]
    state_terms = decays[:, None, :] * batched("jbn,jbe->jne", write_coef, scaled)
    adjoint_terms = factor * batched("jbn,jbe->jne", read_coef, weighted)

    def forward(state, item):
        return (item[0][None, :] * state + item[1], state)

    def backward(adjoint, item):
        return (item[1] + item[0][None, :] * adjoint, adjoint)

    zero_state = jnp.zeros((nstate, channels), jnp.float32)
    state_end, state_local = lax.scan(forward, zero_state, (decays, state_terms))
    adjoint_start, adjoint_local = lax.scan(
        backward, zero_state, (decays, adjoint_terms), reverse=True
    )
    device_decay = jnp.prod(decays, axis=0)
    ones_row = jnp.ones((1, channels), jnp.float32)
    before = jnp.concatenate([ones_row, jnp.cumprod(decays, axis=0)[:-1]], axis=0)
    after = jnp.flip(
        jnp.concatenate([ones_row, jnp.cumprod(jnp.flip(decays, 0), axis=0)[:-1]], axis=0), 0
    )
    identity = (jnp.ones_like(device_decay), zero_state)
    _, state_in = carried_in((device_decay, state_end), "ctx", combine, identity, False)
    _, adjoint_in = carried_in((device_decay, adjoint_start), "ctx", combine, identity, True)
    state_at = (state_local + before[:, None, :] * state_in[None]).astype(jnp.bfloat16)
    adjoint_at = adjoint_local + after[:, None, :] * adjoint_in[None]
    carried = (decays[:, None, :] * adjoint_at).astype(jnp.bfloat16)
    lower_mask = jnp.tril(jnp.ones((BLK, BLK), dtype=bool))
    read_write = jnp.where(
        lower_mask[None], batched("jbn,jcn->jbc", read_coef, write_coef), 0.0
    ).astype(jnp.bfloat16)
    grad_cross = jnp.where(lower_mask[None], batched("jbe,jce->jbc", weighted, scaled), 0.0)
    scan_grad = (
        input_scale[None, None, :]
        / within
        * (
            factor * batched("jbc,jbe->jce", read_write, weighted)
            + batched("jcn,jne->jce", write_coef, carried)
        )
    )
    grad_write = factor * precise("jbc,jbn->jcn", grad_cross, read_wide) + batched(
        "jce,jne->jcn", scaled, carried
    )
    grad_read = factor * (
        batched("jbe,jne->jbn", weighted, state_at)
        + precise("jbc,jcn->jbn", grad_cross, write_wide)
    )
    partial_grad = jnp.concatenate([grad_write, grad_read], axis=2).reshape(length, 2 * nstate)
    grad_coef = lax.psum(partial_grad, "fsdp")
    grad_short = grad_coef.astype(jnp.bfloat16)
    back_grad = jnp.dot(grad_short, proj_weight, preferred_element_type=jnp.float32)
    input_grad = (
        scan_grad.reshape(length, channels)
        + skip[None, :] * upstream_f.reshape(length, channels)
        + back_grad
    ).astype(jnp.bfloat16)
    local_proj = lax.dot_general(
        grad_coef,
        inner.astype(jnp.float32),
        (((0,), (0,)), ((), ())),
        precision=lax.Precision.HIGHEST,
        preferred_element_type=jnp.float32,
    )
    proj_total = lax.psum(local_proj, "ctx")
    return (input_grad, proj_total / (length * lax.axis_size("ctx")))


def solution(mesh):
    placed = (P("ctx", "fsdp"), P(None, "fsdp"), P("fsdp"), P("ctx"), P("fsdp"), P("ctx", "fsdp"))
    return jax.shard_map(
        local,
        mesh=mesh,
        in_specs=placed,
        out_specs=(P("ctx", "fsdp"), P(None, "fsdp")),
        check_vma=False,
    )
```

profile of v0, /device:TPU:0, one launch (start us, length us, event | category | flops | bytes accessed | tf_op | source)
XLA Modules:
  0.0 252.1 jit_solution(15752679022758044592)
XLA Ops:
  8.1 6.7 %fusion.49 = f32[2048,32]{0,1:T(8,128)} fusion(bf16[2048,2048]{1,0:T(8,128)(2,1)} %param.14, bf16[32,2048]{1,0:T(8,128)(2,1)S(1)} %copy-done), kind=kOutput, calls=%fused_computation.70 | convolution fusion | flops 268435456 | bytes 8781824 | tf_op jit(solution)/shard_map/dot_general | solution.py:46
  16.2 16.4 %fusion.4 = (bf16[8,256,2048]{2,1,0:T(8,128)(2,1)}, bf16[8,256,2048]{2,1,0:T(8,128)(2,1)S(1)}, f32[8,256,2048]{2,1,0:T(8,128)}) fusion(bf16[8,256,2048]{2,1,0:T(8,128)(2,1)} %bitcast.83, f32[8,256]{1,0:T(8,128)S(1)} %multiply_bitcast_fusion, f32[256,2048]{1,0:T(8,128)S(1)} %multiply_exponential_fusion, f32[2048]{0:T(1024)S(1)} %negate_sqrt_fusion, ...), kind=kLoop, calls=%fused_computation.17 | loop fusion | flops 33554432 | bytes 52445184 | tf_op jit(solution)/shard_map/convert_element_type | solution.py:66
  32.6 10.1 %fusion.50 = f32[8,256,256]{2,1,0:T(8,128)} fusion(bf16[8,256,2048]{2,1,0:T(8,128)(2,1)S(1)} %get-tuple-element.481, bf16[8,256,2048]{2,1,0:T(8,128)(2,1)} %get-tuple-element.480), kind=kOutput, calls=%fused_computation.71 | convolution fusion | flops 2147483648 | bytes 18874368 | tf_op jit(solution)/shard_map/jbe,jce->jbc/dot_general | solution.py:28
  42.7 1.1 slice_reduce_fusion.1
  44.2 10.7 %all-gather.1 = f32[16384]{0:T(1024)S(1)} all-gather(f32[2048]{0:T(1024)S(1)} %get-tuple-element.478), channel_id=3, replica_groups=mesh['ctx'=8,'fsdp'=4] {'ctx'}, dimensions={0}, use_global_device_ids=true | all-gather | bytes 73728 | tf_op jit(solution)/shard_map/all_gather | solution.py:11
  56.4 5.6 %convolution_multiply_fusion.1 = f32[8,16,2048]{2,1,0:T(8,128)} fusion(bf16[8,256,2048]{2,1,0:T(8,128)(2,1)} %copy-done.1, bf16[8,256,16]{1,0,2:T(8,128)(2,1)S(1)} %get-tuple-element.486), kind=kOutput, calls=%fused_computation.24 | convolution fusion | flops 134479872 | bytes 9502720 | tf_op jit(solution)/shard_map/jbn,jbe->jne/dot_general | solution.py:28
  62.0 8.3 %while.60 = (s32[]{:T(128)}, f32[16,2048]{1,0:T(8,128)S(1)}, f32[8,16,2048]{2,1,0:T(8,128)S(1)}, f32[8,16,2048]{2,1,0:T(8,128)}, f32[8,2048]{1,0:T(8,128)S(1)}, /*index=5*/s32[]{:T(128)}, s32[]{:T(128)}, s32[]{:T(128)}) while((s32[]{:T(128)}, f32[16,2048]{1,0:T(8,128)S(1)}, f32[8,16,2048]{2,1,0:T(8,128)S(1)}, ...), condition=%wide.region_4.5_spmd.clone, body=%wide.region_3.4_spmd.clone.sunk | while | flops 131076 | bytes 680056 | solution.py:80
  62.1 1.0 bitcast_add_fusion.7
  63.1 1.0 bitcast_add_fusion.7
  64.2 1.0 bitcast_add_fusion.7
  65.2 1.0 bitcast_add_fusion.7
  66.3 1.0 bitcast_add_fusion.7
  67.3 1.0 bitcast_add_fusion.7
  68.3 1.0 bitcast_add_fusion.7
  69.4 1.0 bitcast_add_fusion.7
  71.5 5.6 %convolution_multiply_fusion = f32[8,16,2048]{2,1,0:T(8,128)} fusion(bf16[8,256,2048]{2,1,0:T(8,128)(2,1)} %get-tuple-element.480, f32[8,2048]{1,0:T(8,128)S(1)} %get-tuple-element.713, bf16[8,256,16]{1,0,2:T(8,128)(2,1)S(1)} %get-tuple-element.485), kind=kOutput, calls=%fused_computation.23 | convolution fusion | flops 134479872 | bytes 9568256 | tf_op jit(solution)/shard_map/jbn,jbe->jne/dot_general | solution.py:28
  77.1 8.3 %while.62 = (s32[]{:T(128)}, f32[16,2048]{1,0:T(8,128)S(1)}, f32[8,16,2048]{2,1,0:T(8,128)S(1)}, f32[8,2048]{1,0:T(8,128)S(1)}, f32[8,16,2048]{2,1,0:T(8,128)}, /*index=5*/s32[]{:T(128)}, s32[]{:T(128)}) while((s32[]{:T(128)}, f32[16,2048]{1,0:T(8,128)S(1)}, f32[8,16,2048]{2,1,0:T(8,128)S(1)}, f32[8,2048]{1,0:T(8,128)S(1)}, ...), condition=%wide.region_10.11_spmd.clone, body=%wide.region_9.10_spmd.clone.sunk | while | flops 131075 | bytes 680036 | solution.py:79
  77.2 1.0 bitcast_add_fusion.8
  78.2 1.0 bitcast_add_fusion.8
  79.3 1.0 bitcast_add_fusion.8
  80.3 1.0 bitcast_add_fusion.8
  81.4 1.0 bitcast_add_fusion.8
  82.4 1.0 bitcast_add_fusion.8
  83.4 1.0 bitcast_add_fusion.8
  84.5 1.0 bitcast_add_fusion.8
  85.6 11.2 %fusion.11 = f32[8,256,2048]{2,1,0:T(8,128)} fusion(bf16[8,256,2048]{2,1,0:T(8,128)(2,1)} %copy-done.1, pred[256,256]{1,0:T(8,128)(4,1)S(1)} %iota_compare_fusion, bf16[8,256,16]{1,0,2:T(8,128)(2,1)S(1)} %get-tuple-element.486, bf16[8,256,16]{1,0,2:T(8,128)(2,1)S(1)} %get-tuple-element.485), kind=kOutput, calls=%fused_computation.31 | convolution fusion | flops 2165309440 | bytes 25362432 | tf_op jit(solution)/shard_map/jbc,jbe->jce/dot_general | solution.py:28
  96.9 8.2 %while.61 = (s32[]{:T(128)}, f32[16,2048]{1,0:T(8,128)S(1)}, s32[]{:T(128)}, f32[8,16,2048]{2,1,0:T(8,128)}, f32[8,2048]{1,0:T(8,128)S(1)}, /*index=5*/s32[]{:T(128)}, s32[]{:T(128)}, s32[]{:T(128)}, s32[]{:T(128)}) while((s32[]{:T(128)}, f32[16,2048]{1,0:T(8,128)S(1)}, s32[]{:T(128)}, f32[8,16,2048]{2,1,0:T(8,128)}, ...), condition=%wide.region_8.9_spmd.clone, body=%wide.region_7.8_spmd.clone.sunk | while | flops 131080 | bytes 417959 | solution.py:24
  96.9 1.0 fusion.66
  98.0 1.0 fusion.66
  99.0 1.0 fusion.66
  100.0 1.0 fusion.66
  101.1 1.0 fusion.66
  102.1 1.0 fusion.66
  103.1 1.0 fusion.66
  104.1 1.0 fusion.66
  105.1 15.6 %all-gather.8.cloned.1.call-done = f32[128,2048]{1,0:T(8,128)} async-done(((f32[16,2048]{1,0:T(8,128)}), f32[128,2048]{1,0:T(8,128)}) %all-gather.8.cloned.1.call-update) | async-done | bytes 1048592 | tf_op jit(solution)/shard_map/all_gather | solution.py:11
  120.7 8.1 %while.63 = (s32[]{:T(128)}, f32[16,2048]{1,0:T(8,128)S(1)}, s32[]{:T(128)}, f32[8,16,2048]{2,1,0:T(8,128)}, f32[8,2048]{1,0:T(8,128)S(1)}, /*index=5*/s32[]{:T(128)}, s32[]{:T(128)}) while((s32[]{:T(128)}, f32[16,2048]{1,0:T(8,128)S(1)}, s32[]{:T(128)}, f32[8,16,2048]{2,1,0:T(8,128)}, f32[8,2048]{1,0:T(8,128)S(1)}, ...), condition=%wide.region_13.14_spmd.clone, body=%wide.region_12.13_spmd.clone.sunk | while | flops 131076 | bytes 417897 | solution.py:24
  120.7 1.0 fusion.67
  128.8 5.9 %fusion.46 = f32[8,256,16]{1,2,0:T(8,128)S(1)} fusion(bf16[8,256,2048]{2,1,0:T(8,128)(2,1)} %get-tuple-element.480, f32[8,16,2048]{2,1,0:T(8,128)} %copy-done.8, f32[16,2048]{1,0:T(8,128)S(1)} %get-tuple-element.362, f32[8,2048]{1,0:T(8,128)S(1)} %rev.8, f32[8,2048]{1,0:T(8,128)S(1)} %get-tuple-element.714), kind=kOutput, calls=%fused_computation.67 | convolution fusion | flops 135266304 | bytes 9830400 | tf_op jit(solution)/shard_map/jce,jne->jcn/dot_general | solution.py:28
  134.7 3.1 %fusion.15 = f32[8,256,16]{1,2,0:T(8,128)S(1)} fusion(f32[8,256,16]{1,2,0:T(8,128)S(1)} %fusion.46, f32[8,256,256]{2,1,0:T(8,128)} %fusion.50, pred[256,256]{1,0:T(8,128)(4,1)S(1)} %iota_compare_fusion, f32[8,256,16]{1,0,2:T(8,128)S(1)} %get-tuple-element.483), kind=kOutput, calls=%fused_computation.33 | convolution fusion | flops 101253120 | bytes 2555904 | tf_op jit(solution)/shard_map/jbc,jbn->jcn/dot_general | solution.py:32
  137.8 5.9 %fusion.30 = f32[8,256,16]{1,2,0:T(8,128)S(1)} fusion(bf16[8,256,2048]{2,1,0:T(8,128)(2,1)} %copy-done.1, f32[8,16,2048]{2,1,0:T(8,128)} %copy-done.7, f32[16,2048]{1,0:T(8,128)S(1)} %get-tuple-element.365, f32[8,2048]{1,0:T(8,128)S(1)} %concatenate.10), kind=kOutput, calls=%fused_computation.44 | convolution fusion | flops 135004160 | bytes 9764864 | tf_op jit(solution)/shard_map/jbe,jne->jbn/dot_general | solution.py:28
  143.7 2.0 fusion.21
  146.8 12.0 %fusion.2 = f32[8,256,2048]{2,1,0:T(8,128)} fusion(f32[8,256,2048]{2,1,0:T(8,128)} %fusion.11, f32[8,256]{1,0:T(8,128)S(1)} %multiply_bitcast_fusion, f32[256,2048]{1,0:T(8,128)S(1)} %copy-done.5, f32[2048]{0:T(1024)S(1)} %negate_sqrt_fusion, bf16[8,256,16]{1,0,2:T(8,128)(2,1)S(1)} %get-tuple-element.485, f32[8,16,2048]{2,1,0:T(8,128)} %copy-done.8, ...), kind=kOutput, calls=%fused_computation.15 | convolution fusion | flops 156237824 | bytes 37044224 | tf_op jit(solution)/shard_map/jcn,jne->jce/dot_general | solution.py:28
  158.8 23.2 %all-reduce.8.cloned.1.call-done = f32[2048,32]{0,1:T(8,128)} async-done(((f32[2048,32]{0,1:T(8,128)}), f32[2048,32]{0,1:T(8,128)}) %all-reduce.8.cloned.1.call-update) | async-done | bytes 262160 | tf_op jit(solution)/shard_map/psum | solution.py:116
  182.0 8.4 %fusion.51 = f32[32,2048]{1,0:T(8,128)} fusion(f32[2048,32]{0,1:T(8,128)} %all-reduce.8.cloned.1.call-done, bf16[2048,2048]{1,0:T(8,128)(2,1)} %param.14), kind=kOutput, calls=%fused_computation.72 | convolution fusion | flops 1610612736 | bytes 8912896 | tf_op jit(solution)/shard_map/dot_general | solution.py:124
  190.5 13.2 %fusion.6 = bf16[2048,2048]{1,0:T(8,128)(2,1)} fusion(f32[8,256,2048]{2,1,0:T(8,128)} %fusion.2, bf16[32,2048]{1,0:T(8,128)(2,1)S(1)} %copy-done, f32[2048]{0:T(1024)S(1)} %copy-done.12, bf16[2048,2048]{1,0:T(8,128)(2,1)} %param.19, f32[2048,32]{0,1:T(8,128)S(1)} %copy-done.9), kind=kOutput, calls=%fused_computation.21 | convolution fusion | flops 289472512 | bytes 33955840 | tf_op jit(solution)/shard_map/dot_general | solution.py:118
  203.6 40.3 %all-reduce.10.cloned.1.call-done = f32[32,2048]{1,0:T(8,128)} async-done(((f32[32,2048]{1,0:T(8,128)}), f32[32,2048]{1,0:T(8,128)}) %all-reduce.10.cloned.1.call-update) | async-done | bytes 262160 | tf_op jit(solution)/shard_map/psum | solution.py:131
  243.9 1.7 broadcast_multiply_fusion.1
  (126 shorter events, 13.9 us)
Async XLA Ops:
  7.2 0.9 copy-start
  7.2 7.7 %copy-start.13 = (f32[2048]{0:T(1024)S(1)}, f32[2048]{0:T(1024)}, u32[]{:S(2)}) copy-start(f32[2048]{0:T(1024)} %param.17) | copy-start | bytes 24580
  7.2 8.6 %copy-start.11 = (f32[2048]{0:T(1024)S(1)}, f32[2048]{0:T(1024)}, u32[]{:S(2)}) copy-start(f32[2048]{0:T(1024)} %param.16) | copy-start | bytes 24580
  7.2 48.1 %all-reduce.6.cloned.1.call-start = ((), (), s32[]{:S(2)}) async-start(), calls=%async_computation | async-start | bytes 524288 | tf_op jit(solution)/shard_map/psum | solution.py:49
  14.8 82.1 %all-gather.6.cloned.1.call-start = ((), (), s32[]{:S(2)}) async-start(), calls=%async_computation.3 | async-start | bytes 1179648 | tf_op jit(solution)/shard_map/all_gather | solution.py:11
  16.1 16.4 %copy-start.4 = (f32[256,2048]{1,0:T(8,128)}, f32[256,2048]{1,0:T(8,128)S(1)}, u32[]{:S(2)}) copy-start(f32[256,2048]{1,0:T(8,128)S(1)} %multiply_exponential_fusion) | copy-start | bytes 6291460
  32.5 10.1 %copy-start.1 = (bf16[8,256,2048]{2,1,0:T(8,128)(2,1)}, bf16[8,256,2048]{2,1,0:T(8,128)(2,1)S(1)}, u32[]{:S(2)}) copy-start(bf16[8,256,2048]{2,1,0:T(8,128)(2,1)S(1)} %get-tuple-element.481) | copy-start | bytes 25165828
  70.4 0.7 copy-start.3
  70.4 1.1 copy-start.8
  71.0 14.4 %copy-start.10 = (f32[2048,32]{0,1:T(8,128)S(1)}, f32[2048,32]{0,1:T(8,128)}, u32[]{:S(2)}) copy-start(f32[2048,32]{0,1:T(8,128)} %all-reduce.6.cloned.1.call-done) | copy-start | bytes 786436
  71.1 49.7 %all-gather.8.cloned.1.call-start = ((), (), s32[]{:S(2)}) async-start(), calls=%async_computation.4 | async-start | bytes 1179648 | tf_op jit(solution)/shard_map/all_gather | solution.py:11
  85.5 11.3 %copy-start.2 = (f32[16,2048]{1,0:T(8,128)}, f32[16,2048]{1,0:T(8,128)S(1)}, u32[]{:S(2)}) copy-start(f32[16,2048]{1,0:T(8,128)S(1)} %get-tuple-element.364) | copy-start | bytes 393220
  85.5 11.3 %copy-start.7 = (f32[8,16,2048]{2,1,0:T(8,128)}, f32[8,16,2048]{2,1,0:T(8,128)S(1)}, u32[]{:S(2)}) copy-start(f32[8,16,2048]{2,1,0:T(8,128)S(1)} %get-tuple-element.363) | copy-start | bytes 3145732
  96.8 85.2 %all-reduce.8.cloned.1.call-start = ((), (), s32[]{:S(2)}) async-start(), calls=%async_computation.1 | async-start | bytes 524288 | tf_op jit(solution)/shard_map/psum | solution.py:116
  134.7 9.0 %copy-start.6 = (f32[8,256,256]{2,1,0:T(8,128)S(1)}, f32[8,256,256]{2,1,0:T(8,128)}, u32[]{:S(2)}) copy-start(f32[8,256,256]{2,1,0:T(8,128)} %fusion.50) | copy-start | bytes 6291460
  134.7 12.1 %copy-start.5 = (f32[256,2048]{1,0:T(8,128)S(1)}, f32[256,2048]{1,0:T(8,128)}, u32[]{:S(2)}) copy-start(f32[256,2048]{1,0:T(8,128)} %copy-done.4) | copy-start | bytes 6291460
  146.5 97.3 %all-reduce.10.cloned.1.call-start = ((), (), s32[]{:S(2)}) async-start(), calls=%async_computation.2 | async-start | bytes 524288 | tf_op jit(solution)/shard_map/psum | solution.py:131
  158.8 31.7 %copy-start.12 = (f32[2048]{0:T(1024)S(1)}, f32[2048]{0:T(1024)}, u32[]{:S(2)}) copy-start(f32[2048]{0:T(1024)} %param.18) | copy-start | bytes 24580
  182.0 8.5 %copy-start.9 = (f32[2048,32]{0,1:T(8,128)S(1)}, f32[2048,32]{0,1:T(8,128)}, u32[]{:S(2)}) copy-start(f32[2048,32]{0,1:T(8,128)} %all-reduce.8.cloned.1.call-done) | copy-start | bytes 786436
Sparse Core Ops, SparseCore 0:
  14.9 37.9 all-reduce.5
  71.2 23.7 all-gather.5
  97.0 23.6 all-gather.7
  146.7 35.2 all-reduce.7
  190.6 53.2 all-reduce.9
where the time goes:
time: 253 us; the launch traced here: 252 us
  matrix products  89.6 us (35%)
  waiting for transfers between devices  79.2 us (31%)
  other arithmetic  52.9 us (21%)
  between operations  14.1 us (6%)
  blocking collectives  10.7 us (4%)
  local copies, waits for them, and re-layouts  3.93 us (2%)
    dot_general x7, matrix products, batched(): return jnp.einsum(form, left, right, preferred_element_type=jnp.float32)  56.2 us
    psum x1, waiting for transfers between devices, local(): proj_total = lax.psum(local_proj, 'ctx')  40.3 us
    psum x1, waiting for transfers between devices, local(): grad_coef = lax.psum(partial_grad, 'fsdp')  23.2 us
    convert_element_type x1, other arithmetic, local(): scaled = (input_scale[None, None, :] * inner.astype(jnp.float32).reshape(...  16.4 us
    all_gather x2, waiting for transfers between devices, carried_in(): everything = jax.tree.map(lambda part: lax.all_gather(part, axis), shard)  15.6 us
    select_n x16, other arithmetic, step(): return jax.tree.map(lambda a, b: jnp.where(reached, a, b), new, before)  15.6 us
    dot_general x1, matrix products, local(): jnp.dot(grad_short, proj_weight, preferred_element_type=jnp.float32)  13.2 us
    all_gather x1, blocking collectives, carried_in(): everything = jax.tree.map(lambda part: lax.all_gather(part, axis), shard)  10.7 us
  transfers between devices with their start and end apart: 5, of which 3 were waited for; matrix products, arithmetic and copies ran while one was open for 35% of the time, Pallas kernels for 0%

commit v1 on v0

--- a/solution.py
+++ b/solution.py
@@ -128,7 +128,8 @@
         precision=lax.Precision.HIGHEST,
         preferred_element_type=jnp.float32,
     )
-    proj_total = lax.psum(local_proj, "ctx")
+    parts = lax.all_gather(local_proj, "ctx", axis=0, tiled=False)
+    proj_total = parts.sum(axis=0)
     return (input_grad, proj_total / (length * lax.axis_size("ctx")))
 
 

time: 253 us -> 226 us (0.89)
  waiting for transfers between devices: 79.2 us -> 47.2 us
  other arithmetic: 52.9 us -> 58.8 us
    psum x1 -> x0, waiting for transfers between devices: 40.3 us -> none  [local(): proj_total = lax.psum(local_proj, 'ctx')]
    dynamic_update_slice x16, other arithmetic: 0.22 us -> 5.44 us  [local(): lax.scan(forward, zero_state, (decays, state_terms))]
    all_gather x2, waiting for transfers between devices: 15.6 us -> 20.2 us  [carried_in(): everything = jax.tree.map(lambda part: lax.all_gather(part, axis), shard)]
  transfers between devices with their start and end apart: 5 -> 5, of which waited for: 3 -> 4; matrix products, arithmetic and copies ran while one was open for 35% -> 42% of each run, Pallas kernels for 0% -> 0%
where the time goes in v1:
time: 226 us; the launch traced here: 225 us
  matrix products  87.2 us (39%)
  other arithmetic  58.8 us (26%)
  waiting for transfers between devices  47.2 us (21%)
  between operations  14.1 us (6%)
  blocking collectives  10.7 us (5%)
  local copies, waits for them, and re-layouts  5.25 us (2%)
    dot_general x7, matrix products, batched(): return jnp.einsum(form, left, right, preferred_element_type=jnp.float32)  55.5 us
    psum x1, waiting for transfers between devices, local(): grad_coef = lax.psum(partial_grad, 'fsdp')  24.5 us
    all_gather x2, waiting for transfers between devices, carried_in(): everything = jax.tree.map(lambda part: lax.all_gather(part, axis), shard)  20.2 us
    convert_element_type x1, other arithmetic, local(): scaled = (input_scale[None, None, :] * inner.astype(jnp.float32).reshape(...  16.4 us
    select_n x16, other arithmetic, step(): return jax.tree.map(lambda a, b: jnp.where(reached, a, b), new, before)  15.6 us
    dot_general x1, matrix products, local(): jnp.dot(grad_short, proj_weight, preferred_element_type=jnp.float32)  13.3 us
    all_gather x1, blocking collectives, carried_in(): everything = jax.tree.map(lambda part: lax.all_gather(part, axis), shard)  10.7 us
    dot_general x1, matrix products, local(): lax.dot_general(grad_coef, inner.astype(jnp.float32), (((0,), (0,)), ((),...  8.39 us
  transfers between devices with their start and end apart: 5, of which 4 were waited for; matrix products, arithmetic and copies ran while one was open for 42% of the time, Pallas kernels for 0%

profile of v1, /device:TPU:0, one launch (start us, length us, event | category | flops | bytes accessed | tf_op | source)
XLA Modules:
  0.0 225.0 jit_solution(17210717733900846874)
XLA Ops:
  8.1 6.7 %fusion.49 = f32[2048,32]{0,1:T(8,128)} fusion(bf16[2048,2048]{1,0:T(8,128)(2,1)} %param.14, bf16[32,2048]{1,0:T(8,128)(2,1)S(1)} %copy-done), kind=kOutput, calls=%fused_computation.70 | convolution fusion | flops 268435456 | bytes 8781824 | tf_op jit(solution)/shard_map/dot_general | solution.py:46
  16.2 16.4 %fusion.4 = (bf16[8,256,2048]{2,1,0:T(8,128)(2,1)}, bf16[8,256,2048]{2,1,0:T(8,128)(2,1)S(1)}, f32[8,256,2048]{2,1,0:T(8,128)}) fusion(bf16[8,256,2048]{2,1,0:T(8,128)(2,1)} %bitcast.84, f32[8,256]{1,0:T(8,128)S(1)} %multiply_bitcast_fusion, f32[256,2048]{1,0:T(8,128)S(1)} %multiply_exponential_fusion, f32[2048]{0:T(1024)S(1)} %negate_sqrt_fusion, ...), kind=kLoop, calls=%fused_computation.17 | loop fusion | flops 33554432 | bytes 52445184 | tf_op jit(solution)/shard_map/convert_element_type | solution.py:66
  32.6 10.1 %fusion.50 = f32[8,256,256]{2,1,0:T(8,128)} fusion(bf16[8,256,2048]{2,1,0:T(8,128)(2,1)S(1)} %get-tuple-element.481, bf16[8,256,2048]{2,1,0:T(8,128)(2,1)} %get-tuple-element.480), kind=kOutput, calls=%fused_computation.71 | convolution fusion | flops 2147483648 | bytes 18874368 | tf_op jit(solution)/shard_map/jbe,jce->jbc/dot_general | solution.py:28
  42.7 1.1 slice_reduce_fusion.1
  44.2 10.7 %all-gather.1 = f32[16384]{0:T(1024)S(1)} all-gather(f32[2048]{0:T(1024)S(1)} %get-tuple-element.478), channel_id=3, replica_groups=mesh['ctx'=8,'fsdp'=4] {'ctx'}, dimensions={0}, use_global_device_ids=true | all-gather | bytes 73728 | tf_op jit(solution)/shard_map/all_gather | solution.py:11
  56.4 5.6 %convolution_multiply_fusion.1 = f32[8,16,2048]{2,1,0:T(8,128)} fusion(bf16[8,256,2048]{2,1,0:T(8,128)(2,1)} %copy-done.1, bf16[8,256,16]{1,0,2:T(8,128)(2,1)S(1)} %get-tuple-element.486), kind=kOutput, calls=%fused_computation.24 | convolution fusion | flops 134479872 | bytes 9502720 | tf_op jit(solution)/shard_map/jbn,jbe->jne/dot_general | solution.py:28
  62.0 8.3 %while.60 = (s32[]{:T(128)}, f32[16,2048]{1,0:T(8,128)S(1)}, f32[8,16,2048]{2,1,0:T(8,128)S(1)}, f32[8,16,2048]{2,1,0:T(8,128)}, f32[8,2048]{1,0:T(8,128)S(1)}, /*index=5*/s32[]{:T(128)}, s32[]{:T(128)}, s32[]{:T(128)}) while((s32[]{:T(128)}, f32[16,2048]{1,0:T(8,128)S(1)}, f32[8,16,2048]{2,1,0:T(8,128)S(1)}, ...), condition=%wide.region_4.5_spmd.clone, body=%wide.region_3.4_spmd.clone.sunk | while | flops 131076 | bytes 680056 | solution.py:80
  62.1 1.0 bitcast_add_fusion.7
  63.1 1.0 bitcast_add_fusion.7
  64.2 1.0 bitcast_add_fusion.7
  65.2 1.0 bitcast_add_fusion.7
  66.3 1.0 bitcast_add_fusion.7
  67.3 1.0 bitcast_add_fusion.7
  68.3 1.0 bitcast_add_fusion.7
  69.4 1.0 bitcast_add_fusion.7
  71.1 5.7 %convolution_multiply_fusion = f32[8,16,2048]{2,1,0:T(8,128)} fusion(bf16[8,256,2048]{2,1,0:T(8,128)(2,1)} %get-tuple-element.480, f32[8,2048]{1,0:T(8,128)S(1)} %get-tuple-element.713, bf16[8,256,16]{1,0,2:T(8,128)(2,1)S(1)} %get-tuple-element.485), kind=kOutput, calls=%fused_computation.23 | convolution fusion | flops 134479872 | bytes 9568256 | tf_op jit(solution)/shard_map/jbn,jbe->jne/dot_general | solution.py:28
  76.8 1.1 broadcast.46.clone.1
  77.9 13.4 %while.62 = (s32[]{:T(128)}, f32[16,2048]{1,0:T(8,128)S(1)}, f32[8,16,2048]{2,1,0:T(8,128)}, f32[8,2048]{1,0:T(8,128)S(1)}, f32[8,16,2048]{2,1,0:T(8,128)}, /*index=5*/s32[]{:T(128)}, s32[]{:T(128)}) while((s32[]{:T(128)}, f32[16,2048]{1,0:T(8,128)S(1)}, f32[8,16,2048]{2,1,0:T(8,128)}, f32[8,2048]{1,0:T(8,128)S(1)}, ...), condition=%wide.region_10.11_spmd.clone, body=%wide.region_9.10_spmd.clone.sunk | while | flops 131075 | bytes 680544 | solution.py:79
  78.5 1.0 bitcast_add_fusion.8
  80.2 1.0 bitcast_add_fusion.8
  81.9 1.0 bitcast_add_fusion.8
  83.6 1.0 bitcast_add_fusion.8
  85.2 1.0 bitcast_add_fusion.8
  86.9 1.0 bitcast_add_fusion.8
  88.6 1.0 bitcast_add_fusion.8
  90.3 1.0 bitcast_add_fusion.8
  92.2 2.8 %all-gather.8.cloned.1.call-done = f32[128,2048]{1,0:T(8,128)} async-done(((f32[16,2048]{1,0:T(8,128)}), f32[128,2048]{1,0:T(8,128)}) %all-gather.8.cloned.1.call-update) | async-done | bytes 1048592 | tf_op jit(solution)/shard_map/all_gather | solution.py:11
  95.0 8.2 %while.61 = (s32[]{:T(128)}, f32[16,2048]{1,0:T(8,128)S(1)}, s32[]{:T(128)}, f32[8,16,2048]{2,1,0:T(8,128)}, f32[8,2048]{1,0:T(8,128)S(1)}, /*index=5*/s32[]{:T(128)}, s32[]{:T(128)}, s32[]{:T(128)}, s32[]{:T(128)}) while((s32[]{:T(128)}, f32[16,2048]{1,0:T(8,128)S(1)}, s32[]{:T(128)}, f32[8,16,2048]{2,1,0:T(8,128)}, ...), condition=%wide.region_8.9_spmd.clone, body=%wide.region_7.8_spmd.clone.sunk | while | flops 131080 | bytes 417959 | solution.py:24
  95.0 1.0 fusion.66
  96.0 1.0 fusion.66
  98.1 1.0 fusion.66
  99.1 1.0 fusion.66
  100.1 1.0 fusion.66
  101.2 1.0 fusion.66
  102.2 1.0 fusion.66
  103.2 17.4 %all-gather.10.cloned.1.call-done = f32[128,2048]{1,0:T(8,128)} async-done(((f32[16,2048]{1,0:T(8,128)}), f32[128,2048]{1,0:T(8,128)}) %all-gather.10.cloned.1.call-update) | async-done | bytes 1048592 | tf_op jit(solution)/shard_map/all_gather | solution.py:11
  120.6 8.1 %while.63 = (s32[]{:T(128)}, f32[16,2048]{1,0:T(8,128)S(1)}, s32[]{:T(128)}, f32[8,16,2048]{2,1,0:T(8,128)}, f32[8,2048]{1,0:T(8,128)S(1)}, /*index=5*/s32[]{:T(128)}, s32[]{:T(128)}) while((s32[]{:T(128)}, f32[16,2048]{1,0:T(8,128)S(1)}, s32[]{:T(128)}, f32[8,16,2048]{2,1,0:T(8,128)}, f32[8,2048]{1,0:T(8,128)S(1)}, ...), condition=%wide.region_13.14_spmd.clone, body=%wide.region_12.13_spmd.clone.sunk | while | flops 131076 | bytes 417897 | solution.py:24
  128.7 5.8 %fusion.46 = f32[8,256,16]{1,2,0:T(8,128)S(1)} fusion(bf16[8,256,2048]{2,1,0:T(8,128)(2,1)} %get-tuple-element.480, f32[8,16,2048]{2,1,0:T(8,128)S(1)} %get-tuple-element.360, f32[16,2048]{1,0:T(8,128)S(1)} %get-tuple-element.362, f32[8,2048]{1,0:T(8,128)S(1)} %rev.8, f32[8,2048]{1,0:T(8,128)S(1)} %get-tuple-element.714), kind=kOutput, calls=%fused_computation.67 | convolution fusion | flops 135266304 | bytes 9830400 | tf_op jit(solution)/shard_map/jce,jne->jcn/dot_general | solution.py:28
  134.5 5.7 %fusion.30 = f32[8,256,16]{1,2,0:T(8,128)S(1)} fusion(bf16[8,256,2048]{2,1,0:T(8,128)(2,1)} %copy-done.1, f32[8,16,2048]{2,1,0:T(8,128)S(1)} %copy-done.8, f32[16,2048]{1,0:T(8,128)S(1)} %get-tuple-element.365, f32[8,2048]{1,0:T(8,128)S(1)} %concatenate.10), kind=kOutput, calls=%fused_computation.44 | convolution fusion | flops 135004160 | bytes 9764864 | tf_op jit(solution)/shard_map/jbe,jne->jbn/dot_general | solution.py:28
  140.2 1.4 fusion.15
  141.6 2.0 fusion.21
  144.6 10.7 %fusion.11 = f32[8,256,2048]{2,1,0:T(8,128)} fusion(bf16[8,256,2048]{2,1,0:T(8,128)(2,1)} %copy-done.1, pred[256,256]{1,0:T(8,128)(4,1)S(1)} %iota_compare_fusion, bf16[8,256,16]{1,0,2:T(8,128)(2,1)S(1)} %get-tuple-element.486, bf16[8,256,16]{1,0,2:T(8,128)(2,1)S(1)} %get-tuple-element.485), kind=kOutput, calls=%fused_computation.31 | convolution fusion | flops 2165309440 | bytes 25362432 | tf_op jit(solution)/shard_map/jbc,jbe->jce/dot_general | solution.py:28
  155.3 24.5 %all-reduce.7.cloned.1.call-done = f32[2048,32]{0,1:T(8,128)} async-done(((f32[2048,32]{0,1:T(8,128)}), f32[2048,32]{0,1:T(8,128)}) %all-reduce.7.cloned.1.call-update) | async-done | bytes 262160 | tf_op jit(solution)/shard_map/psum | solution.py:116
  179.8 8.4 %fusion.51 = f32[32,2048]{1,0:T(8,128)} fusion(f32[2048,32]{0,1:T(8,128)} %all-reduce.7.cloned.1.call-done, bf16[2048,2048]{1,0:T(8,128)(2,1)} %param.14), kind=kOutput, calls=%fused_computation.72 | convolution fusion | flops 1610612736 | bytes 8912896 | tf_op jit(solution)/shard_map/dot_general | solution.py:124
  188.3 12.0 %fusion.2 = f32[8,256,2048]{2,1,0:T(8,128)} fusion(f32[8,256,2048]{2,1,0:T(8,128)} %fusion.11, f32[8,256]{1,0:T(8,128)S(1)} %multiply_bitcast_fusion, f32[256,2048]{1,0:T(8,128)S(1)} %copy-done.5, f32[2048]{0:T(1024)S(1)} %negate_sqrt_fusion, bf16[8,256,16]{1,0,2:T(8,128)(2,1)S(1)} %get-tuple-element.485, f32[8,16,2048]{2,1,0:T(8,128)} %copy-done.7, ...), kind=kOutput, calls=%fused_computation.15 | convolution fusion | flops 156237824 | bytes 37044224 | tf_op jit(solution)/shard_map/jcn,jne->jce/dot_general | solution.py:28
  200.2 13.3 %fusion.6 = bf16[2048,2048]{1,0:T(8,128)(2,1)} fusion(f32[8,256,2048]{2,1,0:T(8,128)} %fusion.2, bf16[32,2048]{1,0:T(8,128)(2,1)S(1)} %copy-done, f32[2048]{0:T(1024)S(1)} %copy-done.12, bf16[2048,2048]{1,0:T(8,128)(2,1)} %param.19, f32[2048,32]{0,1:T(8,128)S(1)} %copy-done.9), kind=kOutput, calls=%fused_computation.21 | convolution fusion | flops 289472512 | bytes 33955840 | tf_op jit(solution)/shard_map/dot_general | solution.py:118
  213.5 2.5 %all-gather.12.cloned.1.call-done = f32[256,2048]{1,0:T(8,128)} async-done(((f32[32,2048]{1,0:T(8,128)}), f32[256,2048]{1,0:T(8,128)}) %all-gather.12.cloned.1.call-update) | async-done | bytes 2097168 | tf_op jit(solution)/shard_map/all_gather | solution.py:131
  216.0 1.7 reduce_sum.9
  (127 shorter events, 22.0 us)
Async XLA Ops:
  7.2 0.9 copy-start
  7.2 7.7 %copy-start.13 = (f32[2048]{0:T(1024)S(1)}, f32[2048]{0:T(1024)}, u32[]{:S(2)}) copy-start(f32[2048]{0:T(1024)} %param.17) | copy-start | bytes 24580
  7.2 8.6 %copy-start.11 = (f32[2048]{0:T(1024)S(1)}, f32[2048]{0:T(1024)}, u32[]{:S(2)}) copy-start(f32[2048]{0:T(1024)} %param.16) | copy-start | bytes 24580
  7.2 48.1 %all-reduce.5.cloned.1.call-start = ((), (), s32[]{:S(2)}) async-start(), calls=%async_computation | async-start | bytes 524288 | tf_op jit(solution)/shard_map/psum | solution.py:49
  14.8 80.2 %all-gather.8.cloned.1.call-start = ((), (), s32[]{:S(2)}) async-start(), calls=%async_computation.2 | async-start | bytes 1179648 | tf_op jit(solution)/shard_map/all_gather | solution.py:11
  16.1 16.4 %copy-start.4 = (f32[256,2048]{1,0:T(8,128)}, f32[256,2048]{1,0:T(8,128)S(1)}, u32[]{:S(2)}) copy-start(f32[256,2048]{1,0:T(8,128)S(1)} %multiply_exponential_fusion) | copy-start | bytes 6291460
  32.5 10.1 %copy-start.1 = (bf16[8,256,2048]{2,1,0:T(8,128)(2,1)}, bf16[8,256,2048]{2,1,0:T(8,128)(2,1)S(1)}, u32[]{:S(2)}) copy-start(bf16[8,256,2048]{2,1,0:T(8,128)(2,1)S(1)} %get-tuple-element.481) | copy-start | bytes 25165828
  70.4 0.7 copy-start.3
  70.4 58.3 %copy-start.7 = (f32[8,16,2048]{2,1,0:T(8,128)}, f32[8,16,2048]{2,1,0:T(8,128)S(1)}, u32[]{:S(2)}) copy-start(f32[8,16,2048]{2,1,0:T(8,128)S(1)} %get-tuple-element.360) | copy-start | bytes 3145732
  71.0 20.2 %copy-start.10 = (f32[2048,32]{0,1:T(8,128)S(1)}, f32[2048,32]{0,1:T(8,128)}, u32[]{:S(2)}) copy-start(f32[2048,32]{0,1:T(8,128)} %all-reduce.5.cloned.1.call-done) | copy-start | bytes 786436
  71.1 49.5 %all-gather.10.cloned.1.call-start = ((), (), s32[]{:S(2)}) async-start(), calls=%async_computation.3 | async-start | bytes 1179648 | tf_op jit(solution)/shard_map/all_gather | solution.py:11
  91.3 0.7 copy-start.2
  91.9 42.6 %copy-start.8 = (f32[8,16,2048]{2,1,0:T(8,128)S(1)}, f32[8,16,2048]{2,1,0:T(8,128)}, u32[]{:S(2)}) copy-start(f32[8,16,2048]{2,1,0:T(8,128)} %get-tuple-element.363) | copy-start | bytes 3145732
  91.9 87.9 %all-reduce.7.cloned.1.call-start = ((), (), s32[]{:S(2)}) async-start(), calls=%async_computation.1 | async-start | bytes 524288 | tf_op jit(solution)/shard_map/psum | solution.py:116
  128.7 11.5 %copy-start.6 = (f32[8,256,256]{2,1,0:T(8,128)S(1)}, f32[8,256,256]{2,1,0:T(8,128)}, u32[]{:S(2)}) copy-start(f32[8,256,256]{2,1,0:T(8,128)} %fusion.50) | copy-start | bytes 6291460
  144.3 71.7 %all-gather.12.cloned.1.call-start = ((), (), s32[]{:S(2)}) async-start(), calls=%async_computation.4 | async-start | bytes 2359296 | tf_op jit(solution)/shard_map/all_gather | solution.py:131
  155.3 32.9 %copy-start.5 = (f32[256,2048]{1,0:T(8,128)S(1)}, f32[256,2048]{1,0:T(8,128)}, u32[]{:S(2)}) copy-start(f32[256,2048]{1,0:T(8,128)} %copy-done.4) | copy-start | bytes 6291460
  188.2 12.0 %copy-start.9 = (f32[2048,32]{0,1:T(8,128)S(1)}, f32[2048,32]{0,1:T(8,128)}, u32[]{:S(2)}) copy-start(f32[2048,32]{0,1:T(8,128)} %all-reduce.7.cloned.1.call-done) | copy-start | bytes 786436
  188.2 12.0 %copy-start.12 = (f32[2048]{0:T(1024)S(1)}, f32[2048]{0:T(1024)}, u32[]{:S(2)}) copy-start(f32[2048]{0:T(1024)} %param.18) | copy-start | bytes 24580
Sparse Core Ops, SparseCore 0:
  14.9 37.9 all-reduce.4
  71.2 23.7 all-gather.7
  97.0 23.4 all-gather.9
  144.5 35.2 all-reduce.6
  188.3 27.6 all-gather.11
